TPU v7x, 32 devices: a whole 2x2x4 slice. The times are simulated.
32 devices in a mesh: gx: 8 (over z, core), gy: 4 (over y, x).
Axes of the slice: x: 2, y: 2, z: 4, core: 2. Of those that a mesh axis runs over, the one named last changes fastest.
Arguments:
- right_side: float32 [8, 256, 1024], P(None, 'gx', 'gy'), may hold values from -6 to 6
- conductivity: float32 [8, 256, 1024], P(None, 'gx', 'gy'), may hold values from 0.1 to 1
Outputs:
- solution_field: float32 [8, 256, 1024], P(None, 'gx', 'gy')
- residual: float32 [8, 256, 1024], P(None, 'gx', 'gy')
All inputs are finite; a program needn't handle non-finite values.
Results may differ from a plain program's by a relative error of at most 0.0003.
Values sent between devices are 32-bit elements; how exact they have to be, the bound alone decides.
A program may use at most 64 MiB of HBM per device.

v0:
```python
import jax
import jax.numpy as jnp
from jax import lax
from jax.experimental import pallas as pl
from jax.experimental.pallas import tpu as pltpu
from jax.sharding import PartitionSpec as P

low_bound = 0.4
high_bound = 12.0
cheb_theta = 0.5 * (high_bound + low_bound)
cheb_delta = 0.5 * (high_bound - low_bound)
cheb_sigma = cheb_theta / cheb_delta
rho_first = 1.0 / cheb_sigma
rho_second = 1.0 / (2.0 * cheb_sigma - rho_first)
rho_third = 1.0 / (2.0 * cheb_sigma - rho_second)

HALO = 6
LANES = 128
STRIP = 8
GROUP = 8
STEP = 2
MESH = pl.DeviceIdType.MESH
WAYS = ((-1, 0), (1, 0), (0, -1), (0, 1), (-1, -1), (-1, 1), (1, -1), (1, 1))


def kernel(
    num_x, num_y, r_hbm, c_hbm, x_out, res_out,
    r_in, c_in, rc, coef, step_f, res_f, prec, appl, pre2, img,
    packed, side_in, corner_in, turned, msg, from_x, from_y,
    in_sem, halo_send, halo_recv, x_send, x_recv, y_send, y_recv,
):
    levels, rows, cols = r_in.shape
    wide = cols + LANES
    tiles = rows // GROUP
    me_x = lax.axis_index("gx")
    me_y = lax.axis_index("gy")

    def exists(dx, dy):
        ok = jnp.bool_(True)
        if dx < 0:
            ok = me_x > 0
        if dx > 0:
            ok = me_x < num_x - 1
        if dy < 0:
            ok_y = me_y > 0
            ok = ok_y if dx == 0 else jnp.logical_and(ok, ok_y)
        if dy > 0:
            ok_y = me_y < num_y - 1
            ok = ok_y if dx == 0 else jnp.logical_and(ok, ok_y)
        return ok

    loads = [
        pltpu.make_async_copy(r_hbm, r_in, in_sem.at[0]),
        pltpu.make_async_copy(c_hbm, c_in, in_sem.at[1]),
    ]
    for load in loads:
        load.start()

    barrier = pltpu.get_barrier_semaphore()
    expected = jnp.int32(num_x - 1 + num_y - 1)
    for dx, dy in WAYS[4:]:
        ok = exists(dx, dy)

        @pl.when(ok)
        def _():
            pl.semaphore_signal(
                barrier, inc=1, device_id=(me_x + dx, me_y + dy), device_id_type=MESH
            )

        expected = expected + ok.astype(jnp.int32)
    for k in range(1, num_x):
        pl.semaphore_signal(
            barrier, inc=1, device_id=(lax.rem(me_x + k, num_x), me_y), device_id_type=MESH
        )
    for k in range(1, num_y):
        pl.semaphore_signal(
            barrier, inc=1, device_id=(me_x, lax.rem(me_y + k, num_y)), device_id_type=MESH
        )

    lane = lax.broadcasted_iota(jnp.int32, (levels, LANES), 1)

    for load in loads:
        load.wait()
    for a, source in enumerate((r_in, c_in)):
        for t in range(tiles):
            rc[a, HALO + t * GROUP : HALO + (t + 1) * GROUP, :, 0:cols] = jnp.transpose(
                source[:, t * GROUP : (t + 1) * GROUP, :], (1, 0, 2)
            )
    for side in range(2):
        first_lane = 0 if side == 0 else cols - LANES
        offset = 0 if side == 0 else LANES - STRIP
        for t in range(tiles):
            acc = jnp.zeros((levels, LANES), jnp.float32)
            for a in range(2):
                for g in range(GROUP):
                    place = (a * GROUP + g) * STRIP
                    moved = pltpu.roll(
                        rc[a, HALO + t * GROUP + g, :, first_lane : first_lane + LANES],
                        (place - offset) % LANES,
                        1,
                    )
                    acc = jnp.where((lane >= place) & (lane < place + STRIP), moved, acc)
            packed[side, t] = acc

    pl.semaphore_wait(barrier, expected)

    def halo_copy(way):
        dx, dy = WAYS[way]
        if dy == 0:
            src = rc.at[:, pl.ds(HALO if dx < 0 else rows, HALO), :, pl.ds(0, cols)]
            dst = rc.at[:, pl.ds(HALO + rows if dx < 0 else 0, HALO), :, pl.ds(0, cols)]
        elif dx == 0:
            src = packed.at[0 if dy < 0 else 1]
            dst = side_in.at[0 if dy < 0 else 1]
        else:
            src = packed.at[0 if dy < 0 else 1, 0 if dx < 0 else tiles - 1]
            dst = corner_in.at[way - 4]
        return pltpu.make_async_remote_copy(
            src_ref=src, dst_ref=dst, send_sem=halo_send.at[way], recv_sem=halo_recv.at[way],
            device_id=(me_x + dx, me_y + dy), device_id_type=MESH,
        )

    order = (4, 5, 6, 7, 0, 1, 2, 3)
    for way in order:

        @pl.when(exists(*WAYS[way]))
        def _():
            halo_copy(way).start()

    for way in order:
        dx, dy = WAYS[way]
        absent = jnp.logical_not(exists(-dx, -dy))

        @pl.when(absent)
        def _():
            if dy == 0:
                low = HALO + rows if dx < 0 else 0
                rc[:, low : low + HALO, :, 0:cols] = jnp.zeros(
                    (2, HALO, levels, cols), jnp.float32
                )
            elif dx == 0:
                side_in[0 if dy < 0 else 1] = jnp.zeros((tiles, levels, LANES), jnp.float32)
            else:
                corner_in[way - 4] = jnp.zeros((levels, LANES), jnp.float32)

    for way in order:
        dx, dy = WAYS[way]

        @pl.when(exists(-dx, -dy))
        def _():
            halo_copy(way).wait_recv()

    for row in range(rows + 2 * HALO):
        if row < HALO:
            right, left, g = corner_in[2], corner_in[3], row + GROUP - HALO
        elif row < HALO + rows:
            t, g = divmod(row - HALO, GROUP)
            right, left = side_in[0, t], side_in[1, t]
        else:
            right, left, g = corner_in[0], corner_in[1], row - HALO - rows
        for a in range(2):
            place = (a * GROUP + g) * STRIP
            right_moved = pltpu.roll(right, (LANES - place) % LANES, 1)
            left_moved = pltpu.roll(left, (2 * LANES - STRIP - place) % LANES, 1)
            rc[a, row, :, cols:wide] = jnp.where(
                lane < STRIP, right_moved, jnp.where(lane >= LANES - STRIP, left_moved, 0.0)
            )

    field = rc.at[0]
    cond = rc.at[1]
    level = lax.broadcasted_iota(jnp.int32, (STEP, levels, wide), 1)

    def around(v):
        return (
            pltpu.roll(v, 1, 2),
            pltpu.roll(v, wide - 1, 2),
            pltpu.roll(v, 1, 1),
            pltpu.roll(v, levels - 1, 1),
        )

    def coefficients(x):
        c = cond[pl.ds(x, STEP)]
        west, east, below, above = around(c)
        below = jnp.where(level > 0, below, 0.0)
        above = jnp.where(level < levels - 1, above, 0.0)
        inside = c > 0.0
        faces = [
            jnp.where(inside, 0.5 * (c + other), 0.0)
            for other in (cond[pl.ds(x - 1, STEP)], cond[pl.ds(x + 1, STEP)], west, east, below, above)
        ]
        diag = ((faces[0] + faces[1]) + (faces[2] + faces[3])) + (faces[4] + faces[5])
        faces[4] = jnp.where(level > 0, faces[4], 0.0)
        faces[5] = jnp.where(level < levels - 1, faces[5], 0.0)
        return [diag] + faces

    def apply(ref, x, k):
        v = ref[pl.ds(x, STEP)]
        west, east, below, above = around(v)
        off = (
            (k[1] * ref[pl.ds(x - 1, STEP)] + k[2] * ref[pl.ds(x + 1, STEP)])
            + (k[3] * west + k[4] * east)
        ) + (k[5] * below + k[6] * above)
        return v, k[0] * v - off

    def kept(x):
        return [coef[i, pl.ds(x, STEP)] for i in range(7)]

    def sweep(low, body, carry=None):
        def at(i, state):
            return body(low + i * STEP, state)

        return lax.fori_loop(0, (rows + 2 * HALO - 2 * low) // STEP, at, carry)

    def opening(ref, x, k):
        v, image = apply(ref, x, k)
        res_one = v - image * (1.0 / cheb_theta)
        res_f[pl.ds(x, STEP)] = res_one
        step_f[pl.ds(x, STEP)] = (
            (rho_second * rho_first / cheb_theta) * v + (2.0 * rho_second / cheb_delta) * res_one
        )

    def closing(source, out, x):
        step_one, image = apply(step_f, x, kept(x))
        res_two = res_f[pl.ds(x, STEP)] - image
        out[pl.ds(x, STEP)] = (
            (1.0 / cheb_theta) * source[pl.ds(x, STEP)]
            + (1.0 + rho_third * rho_second) * step_one
            + (2.0 * rho_third / cheb_delta) * res_two
        )

    def sweep_one(x, state):
        k = coefficients(x)
        for i in range(7):
            coef[i, pl.ds(x, STEP)] = k[i]
        opening(field, x, k)
        return state

    def sweep_two(x, state):
        closing(field, prec, x)
        return state

    def sweep_three(x, state):
        appl[pl.ds(x, STEP)] = apply(prec, x, kept(x))[1]
        return state

    def sweep_four(x, state):
        opening(appl, x, kept(x))
        return state

    def sweep_five(x, state):
        closing(appl, pre2, x)
        return state

    def folded(v):
        total = v[0]
        for i in range(1, STEP):
            total = total + v[i]
        parts = [total[:, i : i + LANES] for i in range(0, cols, LANES)]
        out = parts[0]
        for part in parts[1:]:
            out = out + part
        return out

    def sweep_six(x, state):
        m_all, n_all = apply(pre2, x, kept(x))
        img[pl.ds(x, STEP)] = n_all[:, :, 0:cols]
        m, n = m_all[:, :, 0:cols], n_all[:, :, 0:cols]
        r = field[pl.ds(x, STEP), :, 0:cols]
        p = prec[pl.ds(x, STEP), :, 0:cols]
        w = appl[pl.ds(x, STEP), :, 0:cols]
        products = (r * p, w * p, r * m, w * m, n * p, n * m)
        return tuple(s + folded(v) for s, v in zip(state, products))

    sweep(1, sweep_one)
    sweep(2, sweep_two)
    sweep(3, sweep_three)
    sweep(4, sweep_four)
    sweep(5, sweep_five)
    zero = jnp.zeros((levels, LANES), jnp.float32)
    sums = sweep(6, sweep_six, (zero,) * 6)

    line = lax.broadcasted_iota(jnp.int32, (8, LANES), 0)
    table = jnp.zeros((8, LANES), jnp.float32)
    for i, s in enumerate(sums):
        table = jnp.where(line == i, jnp.sum(s, axis=0, keepdims=True), table)
    msg[0] = table

    def turn(slot, ref):
        for t in range(tiles):
            turned[slot, :, t * GROUP : (t + 1) * GROUP, :] = jnp.transpose(
                ref[HALO + t * GROUP : HALO + (t + 1) * GROUP, :, 0:cols], (1, 0, 2)
            )

    copies = []
    for k in range(1, num_x):
        copies.append(pltpu.make_async_remote_copy(
            src_ref=msg.at[0], dst_ref=from_x.at[k - 1],
            send_sem=x_send.at[k - 1], recv_sem=x_recv.at[k - 1],
            device_id=(lax.rem(me_x + k, num_x), me_y), device_id_type=MESH,
        ))
    for copy in copies:
        copy.start()
    turn(0, prec)
    turn(1, appl)
    for copy in copies:
        copy.wait_recv()
    total = msg[0]
    for k in range(1, num_x):
        total = total + from_x[k - 1]
    msg[1] = total
    more = []
    for k in range(1, num_y):
        more.append(pltpu.make_async_remote_copy(
            src_ref=msg.at[1], dst_ref=from_y.at[k - 1],
            send_sem=y_send.at[k - 1], recv_sem=y_recv.at[k - 1],
            device_id=(me_x, lax.rem(me_y + k, num_y)), device_id_type=MESH,
        ))
    for copy in more:
        copy.start()
    turn(2, pre2)
    turn(3, img)
    for copy in more:
        copy.wait_recv()
    total = msg[1]
    for k in range(1, num_y):
        total = total + from_y[k - 1]

    def lanes_of(i):
        return total[i : i + 1, :]

    rp, wp, rm, wm, np_, nm = (lanes_of(i) for i in range(6))
    gamma_old = jnp.sum(rp, axis=1, keepdims=True)
    alpha_old = gamma_old / jnp.sum(wp, axis=1, keepdims=True)
    gamma = jnp.sum((rp - alpha_old * wp) - alpha_old * (rm - alpha_old * wm), axis=1, keepdims=True)
    delta = jnp.sum((wp - alpha_old * np_) - alpha_old * (wm - alpha_old * nm), axis=1, keepdims=True)
    beta = gamma / gamma_old
    alpha = gamma / (delta - beta * gamma / alpha_old)
    near = alpha_old + alpha * (1.0 + beta)
    far = alpha * alpha_old
    for z in range(levels):
        x_out[z] = near * turned[0, z] - far * turned[2, z]
        res_out[z] = (r_in[z] - near * turned[1, z]) + far * turned[3, z]

    for way in order:

        @pl.when(exists(*WAYS[way]))
        def _():
            halo_copy(way).wait_send()

    for copy in copies + more:
        copy.wait_send()


def solution(mesh):
    num_x, num_y = mesh.shape["gx"], mesh.shape["gy"]

    def per_device(right_side, conductivity):
        levels, rows, cols = right_side.shape
        high = rows + 2 * HALO
        wide = cols + LANES
        tiles = rows // GROUP

        def body(*refs):
            kernel(num_x, num_y, *refs)

        block = (levels, rows, cols)
        full = (high, levels, wide)
        out = jax.ShapeDtypeStruct(block, jnp.float32)
        vmem = lambda shape: pltpu.VMEM(shape, jnp.float32)
        dma = lambda n: pltpu.SemaphoreType.DMA((n,))
        return pl.pallas_call(
            body,
            out_shape=(out, out),
            in_specs=[pl.BlockSpec(memory_space=pl.ANY)] * 2,
            out_specs=(pl.BlockSpec(memory_space=pltpu.VMEM),) * 2,
            scratch_shapes=[
                vmem(block), vmem(block), vmem((2,) + full), vmem((7,) + full),
                vmem(full), vmem(full), vmem(full), vmem(full), vmem(full),
                vmem((high, levels, cols)),
                vmem((2, tiles, levels, LANES)), vmem((2, tiles, levels, LANES)),
                vmem((4, levels, LANES)), vmem((4,) + block),
                vmem((2, 8, LANES)), vmem((max(num_x - 1, 1), 8, LANES)),
                vmem((max(num_y - 1, 1), 8, LANES)),
                dma(2), dma(8), dma(8),
                dma(max(num_x - 1, 1)), dma(max(num_x - 1, 1)),
                dma(max(num_y - 1, 1)), dma(max(num_y - 1, 1)),
            ],
            compiler_params=pltpu.CompilerParams(
                collective_id=0, has_side_effects=True, vmem_limit_bytes=32 * 1024 * 1024
            ),
        )(right_side, conductivity)

    return jax.shard_map(
        per_device,
        mesh=mesh,
        in_specs=(P(None, "gx", "gy"), P(None, "gx", "gy")),
        out_specs=(P(None, "gx", "gy"), P(None, "gx", "gy")),
        check_vma=False,
    )
```

profile of v0, /device:TPU:0, one launch (start us, length us, event | category | flops | bytes accessed | tf_op | source)
XLA Modules:
  0.0 30.4 jit_solution(11313176908049652643)
XLA Ops:
  0.6 0.0 copy-start
  0.6 0.9 %copy-done = f32[8,32,256]{2,1,0:T(8,128)S(1)} copy-done((f32[8,32,256]{2,1,0:T(8,128)S(1)}, f32[8,32,256]{2,1,0:T(8,128)}, u32[]{:S(2)}) %copy-start) | copy-done | bytes 262168
  1.6 0.0 copy-start.1
  1.6 0.9 %copy-done.1 = f32[8,32,256]{2,1,0:T(8,128)S(1)} copy-done((f32[8,32,256]{2,1,0:T(8,128)S(1)}, f32[8,32,256]{2,1,0:T(8,128)}, u32[]{:S(2)}) %copy-start.1) | copy-done | bytes 262168
  2.5 26.4 %shard_map.41 = (f32[8,32,256]{2,1,0:T(8,128)S(1)}, f32[8,32,256]{2,1,0:T(8,128)S(1)}) custom-call(f32[8,32,256]{2,1,0:T(8,128)S(1)} %copy-done, f32[8,32,256]{2,1,0:T(8,128)S(1)} %copy-done.1), custom_call_target="tpu_custom_call" | custom-call | tf_op jit(solution)/shard_map/pallas_call | solution.py:371
  28.9 0.7 %copy.6 = f32[8,32,256]{2,1,0:T(8,128)} copy(f32[8,32,256]{2,1,0:T(8,128)S(1)} %get-tuple-element.4) | data formatting | bytes 524288
  29.7 0.7 %copy.7 = f32[8,32,256]{2,1,0:T(8,128)} copy(f32[8,32,256]{2,1,0:T(8,128)S(1)} %get-tuple-element.5) | data formatting | bytes 524288
Async XLA Ops:
  0.6 1.0 %copy-start = (f32[8,32,256]{2,1,0:T(8,128)S(1)}, f32[8,32,256]{2,1,0:T(8,128)}, u32[]{:S(2)}) copy-start(f32[8,32,256]{2,1,0:T(8,128)} %refs_0_.1) | copy-start | bytes 786436
  1.6 0.9 %copy-start.1 = (f32[8,32,256]{2,1,0:T(8,128)S(1)}, f32[8,32,256]{2,1,0:T(8,128)}, u32[]{:S(2)}) copy-start(f32[8,32,256]{2,1,0:T(8,128)} %refs_1_.1) | copy-start | bytes 786436
where the time goes:
time: 30.5 us; the launch traced here: 30.4 us
  Pallas kernels  26.4 us (87%)
  local copies, waits for them, and re-layouts  3.3 us (11%)
  between operations  0.65 us (2%)
    pallas_call x1, Pallas kernels, per_device(): pl.pallas_call(body, out_shape=(out, out), in_specs=[pl.BlockSpec(memory_...  26.4 us
    unnamed x6, local copies, waits for them, and re-layouts  3.3 us

commit v1 on v0

--- a/solution.py
+++ b/solution.py
@@ -168,8 +168,6 @@
 
     field = rc.at[0]
     cond = rc.at[1]
-    level = lax.broadcasted_iota(jnp.int32, (STEP, levels, wide), 1)
-
     def around(v):
         return (
             pltpu.roll(v, 1, 2),
@@ -178,82 +176,82 @@
             pltpu.roll(v, levels - 1, 1),
         )
 
-    def coefficients(x):
-        c = cond[pl.ds(x, STEP)]
+    def coefficients(x, n):
+        level = lax.broadcasted_iota(jnp.int32, (n, levels, wide), 1)
+        c = cond[pl.ds(x, n)]
         west, east, below, above = around(c)
         below = jnp.where(level > 0, below, 0.0)
         above = jnp.where(level < levels - 1, above, 0.0)
         inside = c > 0.0
         faces = [
             jnp.where(inside, 0.5 * (c + other), 0.0)
-            for other in (cond[pl.ds(x - 1, STEP)], cond[pl.ds(x + 1, STEP)], west, east, below, above)
+            for other in (cond[pl.ds(x - 1, n)], cond[pl.ds(x + 1, n)], west, east, below, above)
         ]
         diag = ((faces[0] + faces[1]) + (faces[2] + faces[3])) + (faces[4] + faces[5])
         faces[4] = jnp.where(level > 0, faces[4], 0.0)
         faces[5] = jnp.where(level < levels - 1, faces[5], 0.0)
         return [diag] + faces
 
-    def apply(ref, x, k):
-        v = ref[pl.ds(x, STEP)]
+    def apply(ref, x, n, k):
+        v = ref[pl.ds(x, n)]
         west, east, below, above = around(v)
         off = (
-            (k[1] * ref[pl.ds(x - 1, STEP)] + k[2] * ref[pl.ds(x + 1, STEP)])
+            (k[1] * ref[pl.ds(x - 1, n)] + k[2] * ref[pl.ds(x + 1, n)])
             + (k[3] * west + k[4] * east)
         ) + (k[5] * below + k[6] * above)
         return v, k[0] * v - off
 
-    def kept(x):
-        return [coef[i, pl.ds(x, STEP)] for i in range(7)]
+    def kept(x, n):
+        return [coef[i, pl.ds(x, n)] for i in range(7)]
 
     def sweep(low, body, carry=None):
-        def at(i, state):
-            return body(low + i * STEP, state)
-
-        return lax.fori_loop(0, (rows + 2 * HALO - 2 * low) // STEP, at, carry)
-
-    def opening(ref, x, k):
-        v, image = apply(ref, x, k)
+        count, rest = divmod(rows + 2 * HALO - 2 * low, STEP)
+        carry = lax.fori_loop(0, count, lambda i, s: body(low + i * STEP, STEP, s), carry)
+        return body(low + count * STEP, rest, carry) if rest else carry
+
+    def opening(ref, x, n, k):
+        v, image = apply(ref, x, n, k)
         res_one = v - image * (1.0 / cheb_theta)
-        res_f[pl.ds(x, STEP)] = res_one
-        step_f[pl.ds(x, STEP)] = (
+        res_f[pl.ds(x, n)] = res_one
+        step_f[pl.ds(x, n)] = (
             (rho_second * rho_first / cheb_theta) * v + (2.0 * rho_second / cheb_delta) * res_one
         )
 
-    def closing(source, out, x):
-        step_one, image = apply(step_f, x, kept(x))
-        res_two = res_f[pl.ds(x, STEP)] - image
-        out[pl.ds(x, STEP)] = (
-            (1.0 / cheb_theta) * source[pl.ds(x, STEP)]
+    def closing(source, out, x, n):
+        step_one, image = apply(step_f, x, n, kept(x, n))
+        res_two = res_f[pl.ds(x, n)] - image
+        out[pl.ds(x, n)] = (
+            (1.0 / cheb_theta) * source[pl.ds(x, n)]
             + (1.0 + rho_third * rho_second) * step_one
             + (2.0 * rho_third / cheb_delta) * res_two
         )
 
-    def sweep_one(x, state):
-        k = coefficients(x)
+    def sweep_one(x, n, state):
+        k = coefficients(x, n)
         for i in range(7):
-            coef[i, pl.ds(x, STEP)] = k[i]
-        opening(field, x, k)
-        return state
-
-    def sweep_two(x, state):
-        closing(field, prec, x)
-        return state
-
-    def sweep_three(x, state):
-        appl[pl.ds(x, STEP)] = apply(prec, x, kept(x))[1]
-        return state
-
-    def sweep_four(x, state):
-        opening(appl, x, kept(x))
-        return state
-
-    def sweep_five(x, state):
-        closing(appl, pre2, x)
+            coef[i, pl.ds(x, n)] = k[i]
+        opening(field, x, n, k)
+        return state
+
+    def sweep_two(x, n, state):
+        closing(field, prec, x, n)
+        return state
+
+    def sweep_three(x, n, state):
+        appl[pl.ds(x, n)] = apply(prec, x, n, kept(x, n))[1]
+        return state
+
+    def sweep_four(x, n, state):
+        opening(appl, x, n, kept(x, n))
+        return state
+
+    def sweep_five(x, n, state):
+        closing(appl, pre2, x, n)
         return state
 
     def folded(v):
         total = v[0]
-        for i in range(1, STEP):
+        for i in range(1, v.shape[0]):
             total = total + v[i]
         parts = [total[:, i : i + LANES] for i in range(0, cols, LANES)]
         out = parts[0]
@@ -261,14 +259,14 @@
             out = out + part
         return out
 
-    def sweep_six(x, state):
-        m_all, n_all = apply(pre2, x, kept(x))
-        img[pl.ds(x, STEP)] = n_all[:, :, 0:cols]
-        m, n = m_all[:, :, 0:cols], n_all[:, :, 0:cols]
-        r = field[pl.ds(x, STEP), :, 0:cols]
-        p = prec[pl.ds(x, STEP), :, 0:cols]
-        w = appl[pl.ds(x, STEP), :, 0:cols]
-        products = (r * p, w * p, r * m, w * m, n * p, n * m)
+    def sweep_six(x, n, state):
+        m_all, i_all = apply(pre2, x, n, kept(x, n))
+        img[pl.ds(x, n)] = i_all[:, :, 0:cols]
+        m, q = m_all[:, :, 0:cols], i_all[:, :, 0:cols]
+        r = field[pl.ds(x, n), :, 0:cols]
+        p = prec[pl.ds(x, n), :, 0:cols]
+        w = appl[pl.ds(x, n), :, 0:cols]
+        products = (r * p, w * p, r * m, w * m, q * p, q * m)
         return tuple(s + folded(v) for s, v in zip(state, products))
 
     sweep(1, sweep_one)
@@ -371,7 +369,7 @@
         return pl.pallas_call(
             body,
             out_shape=(out, out),
-            in_specs=[pl.BlockSpec(memory_space=pl.ANY)] * 2,
+            in_specs=[pl.BlockSpec(memory_space=pltpu.HBM)] * 2,
             out_specs=(pl.BlockSpec(memory_space=pltpu.VMEM),) * 2,
             scratch_shapes=[
                 vmem(block), vmem(block), vmem((2,) + full), vmem((7,) + full),
@@ -386,7 +384,7 @@
                 dma(max(num_y - 1, 1)), dma(max(num_y - 1, 1)),
             ],
             compiler_params=pltpu.CompilerParams(
-                collective_id=0, has_side_effects=True, vmem_limit_bytes=32 * 1024 * 1024
+                collective_id=0, has_side_effects=True, vmem_limit_bytes=56000000
             ),
         )(right_side, conductivity)
 

time: 30.5 us -> 28.6 us (0.938)
  local copies, waits for them, and re-layouts: 3.3 us -> 1.41 us
    unnamed x6 -> x2, local copies, waits for them, and re-layouts: 3.3 us -> 1.41 us
where the time goes in v1:
time: 28.6 us; the launch traced here: 28.4 us
  Pallas kernels  26.4 us (92%)
  local copies, waits for them, and re-layouts  1.41 us (5%)
  between operations  0.64 us (2%)
    pallas_call x1, Pallas kernels, per_device(): pl.pallas_call(body, out_shape=(out, out), in_specs=[pl.BlockSpec(memory_...  26.4 us
    unnamed x2, local copies, waits for them, and re-layouts  1.41 us

profile of v1, /device:TPU:0, one launch (start us, length us, event | category | flops | bytes accessed | tf_op | source)
XLA Modules:
  0.0 28.4 jit_solution(9812378755831785525)
XLA Ops:
  0.6 26.4 %shard_map.41 = (f32[8,32,256]{2,1,0:T(8,128)S(1)}, f32[8,32,256]{2,1,0:T(8,128)S(1)}) custom-call(f32[8,32,256]{2,1,0:T(8,128)} %refs_0_.1, f32[8,32,256]{2,1,0:T(8,128)} %refs_1_.1), custom_call_target="tpu_custom_call" | custom-call | tf_op jit(solution)/shard_map/pallas_call | solution.py:369
  27.0 0.7 %copy.6 = f32[8,32,256]{2,1,0:T(8,128)} copy(f32[8,32,256]{2,1,0:T(8,128)S(1)} %get-tuple-element.4) | data formatting | bytes 524288
  27.7 0.7 %copy.7 = f32[8,32,256]{2,1,0:T(8,128)} copy(f32[8,32,256]{2,1,0:T(8,128)S(1)} %get-tuple-element.5) | data formatting | bytes 524288

commit v2 on v1

--- a/solution.py
+++ b/solution.py
@@ -18,7 +18,7 @@
 LANES = 128
 STRIP = 8
 GROUP = 8
-STEP = 2
+STEP = 4
 MESH = pl.DeviceIdType.MESH
 WAYS = ((-1, 0), (1, 0), (0, -1), (0, 1), (-1, -1), (-1, 1), (1, -1), (1, 1))
 

time: 28.6 us -> 24.6 us (0.86)
  Pallas kernels: 26.4 us -> 22.4 us
    pallas_call x1, Pallas kernels: 26.4 us -> 22.4 us  [per_device(): pl.pallas_call(body, out_shape=(out, out), in_specs=[pl.BlockSpec(memory_...]
where the time goes in v2:
time: 24.6 us; the launch traced here: 24.5 us
  Pallas kernels  22.4 us (91%)
  local copies, waits for them, and re-layouts  1.41 us (6%)
  between operations  0.64 us (3%)
    pallas_call x1, Pallas kernels, per_device(): pl.pallas_call(body, out_shape=(out, out), in_specs=[pl.BlockSpec(memory_...  22.4 us
    unnamed x2, local copies, waits for them, and re-layouts  1.41 us

profile of v2, /device:TPU:0, one launch (start us, length us, event | category | flops | bytes accessed | tf_op | source)
XLA Modules:
  0.0 24.5 jit_solution(1123750930316924518)
XLA Ops:
  0.6 22.4 %shard_map.41 = (f32[8,32,256]{2,1,0:T(8,128)S(1)}, f32[8,32,256]{2,1,0:T(8,128)S(1)}) custom-call(f32[8,32,256]{2,1,0:T(8,128)} %refs_0_.1, f32[8,32,256]{2,1,0:T(8,128)} %refs_1_.1), custom_call_target="tpu_custom_call" | custom-call | tf_op jit(solution)/shard_map/pallas_call | solution.py:369
  23.1 0.7 %copy.6 = f32[8,32,256]{2,1,0:T(8,128)} copy(f32[8,32,256]{2,1,0:T(8,128)S(1)} %get-tuple-element.4) | data formatting | bytes 524288
  23.8 0.7 %copy.7 = f32[8,32,256]{2,1,0:T(8,128)} copy(f32[8,32,256]{2,1,0:T(8,128)S(1)} %get-tuple-element.5) | data formatting | bytes 524288

commit v3 on v2

--- a/solution.py
+++ b/solution.py
@@ -18,7 +18,7 @@
 LANES = 128
 STRIP = 8
 GROUP = 8
-STEP = 4
+STEP = 8
 MESH = pl.DeviceIdType.MESH
 WAYS = ((-1, 0), (1, 0), (0, -1), (0, 1), (-1, -1), (-1, 1), (1, -1), (1, 1))
 

time: 24.6 us -> 22.8 us (0.927)
  Pallas kernels: 22.4 us -> 20.6 us
    pallas_call x1, Pallas kernels: 22.4 us -> 20.6 us  [per_device(): pl.pallas_call(body, out_shape=(out, out), in_specs=[pl.BlockSpec(memory_...]
where the time goes in v3:
time: 22.8 us; the launch traced here: 22.6 us
  Pallas kernels  20.6 us (90%)
  local copies, waits for them, and re-layouts  1.41 us (6%)
  between operations  0.64 us (3%)
    pallas_call x1, Pallas kernels, per_device(): pl.pallas_call(body, out_shape=(out, out), in_specs=[pl.BlockSpec(memory_...  20.6 us
    unnamed x2, local copies, waits for them, and re-layouts  1.41 us

profile of v3, /device:TPU:0, one launch (start us, length us, event | category | flops | bytes accessed | tf_op | source)
XLA Modules:
  0.0 22.6 jit_solution(6771089528352456126)
XLA Ops:
  0.6 20.6 %shard_map.41 = (f32[8,32,256]{2,1,0:T(8,128)S(1)}, f32[8,32,256]{2,1,0:T(8,128)S(1)}) custom-call(f32[8,32,256]{2,1,0:T(8,128)} %refs_0_.1, f32[8,32,256]{2,1,0:T(8,128)} %refs_1_.1), custom_call_target="tpu_custom_call" | custom-call | tf_op jit(solution)/shard_map/pallas_call | solution.py:369
  21.2 0.7 %copy.6 = f32[8,32,256]{2,1,0:T(8,128)} copy(f32[8,32,256]{2,1,0:T(8,128)S(1)} %get-tuple-element.4) | data formatting | bytes 524288
  21.9 0.7 %copy.7 = f32[8,32,256]{2,1,0:T(8,128)} copy(f32[8,32,256]{2,1,0:T(8,128)S(1)} %get-tuple-element.5) | data formatting | bytes 524288
